TPU v7x, 32 devices: a whole 2x2x4 slice. The times are simulated.
32 devices in a mesh: inst: 2 (over y), cell: 16 (over z, x, core).
Axes of the slice: x: 2, y: 2, z: 4, core: 2. Of those that a mesh axis runs over, the one named last changes fastest.
Arguments:
- adjoint: bfloat16 [4, 5, 32, 16, 256], P('inst', None, 'cell'), may hold values from -6 to 6
- flux_jac: bfloat16 [4, 5, 3, 32, 16, 256], P('inst', None, None, 'cell'), may hold values from -1.25 to 1.25
- shift: float32 [32, 16, 256], P('cell', 'inst'), may hold values from 0.1 to 2
Outputs:
- mesh_adjoint: float32 [3, 32, 16, 256], P(None, 'cell', 'inst')
- residual: float32 [3, 32, 16, 256], P(None, 'cell', 'inst')
All inputs are finite; a program needn't handle non-finite values.
Results may differ from a plain program's by a relative error of at most 0.0003.
Values may be sent and summed in bfloat16 or wider, within the bound.
A program may use at most 64 MiB of HBM per device.

v0:
```python
import jax
import jax.numpy as jnp
from jax import lax
from jax.sharding import PartitionSpec as P

ITERS = 3
mu_shear = 1.0
lame_first = 1.5


def padded_2(block, sides, width):
    for axis, dim in sides:
        count = lax.axis_size(axis)
        forward = [(i, i + 1) for i in range(count - 1)]
        backward = [(target, source) for source, target in forward]
        low = lax.ppermute(
            lax.slice_in_dim(block, block.shape[dim] - width, None, axis=dim), axis, forward
        )
        high = lax.ppermute(lax.slice_in_dim(block, 0, width, axis=dim), axis, backward)
        block = jnp.concatenate([low, block, high], axis=dim)
    return block


def operate(field, shift):
    padded = padded_2(field, (("inst", 2), ("cell", 1)), 1)
    padded = jnp.pad(padded, ((0, 0), (0, 0), (0, 0), (1, 1)))
    center = padded[:, 1:-1, 1:-1, 1:-1]
    beside = padded[:, 2:, 1:-1, 1:-1] + padded[:, :-2, 1:-1, 1:-1]
    beside = beside + padded[:, 1:-1, 2:, 1:-1] + padded[:, 1:-1, :-2, 1:-1]
    beside = beside + padded[:, 1:-1, 1:-1, 2:] + padded[:, 1:-1, 1:-1, :-2]
    corner = padded[:, :-1, :-1, :-1]
    diverge = (
        padded[0, 1:, :-1, :-1]
        - corner[0]
        + (padded[1, :-1, 1:, :-1] - corner[1])
        + (padded[2, :-1, :-1, 1:] - corner[2])
    )
    cell_first = lax.axis_index("cell") == 0
    inst_first = lax.axis_index("inst") == 0
    keep_rows = jnp.where((jnp.arange(diverge.shape[0]) == 0) & cell_first, 0.0, 1.0).astype(
        jnp.float32
    )
    keep_cols = jnp.where((jnp.arange(diverge.shape[1]) == 0) & inst_first, 0.0, 1.0).astype(
        jnp.float32
    )
    keep_depth = jnp.where(jnp.arange(diverge.shape[2]) == 0, 0.0, 1.0).astype(jnp.float32)
    diverge = (
        diverge * keep_rows[:, None, None] * keep_cols[None, :, None] * keep_depth[None, None, :]
    )
    inner = diverge[1:, 1:, 1:]
    grad_part = jnp.stack(
        [diverge[:-1, 1:, 1:] - inner, diverge[1:, :-1, 1:] - inner, diverge[1:, 1:, :-1] - inner]
    )
    return mu_shear * (6.0 * center - beside) + shift * center + lame_first * grad_part


def two_products(residual, image):
    return lax.psum((jnp.sum(residual * residual), jnp.sum(residual * image)), ("inst", "cell"))


def local(adjoint, flux_jac, shift):
    padded = padded_2(adjoint, (("cell", 2),), 1)
    upper = jnp.einsum(
        "ivkxyz,ivxyz->kxyz", flux_jac, padded[:, :, 2:], preferred_element_type=jnp.float32
    )
    lower = jnp.einsum(
        "ivkxyz,ivxyz->kxyz", flux_jac, padded[:, :, :-2], preferred_element_type=jnp.float32
    )
    partial_sum = upper - lower
    block_cols = shift.shape[1]
    totals = lax.psum(partial_sum, "inst")
    sens = lax.dynamic_slice_in_dim(totals, lax.axis_index("inst") * block_cols, block_cols, 2)
    mesh_adjoint = jnp.zeros_like(sens)
    residual = sens
    image = operate(residual, shift)
    norm_now, product = two_products(residual, image)
    alpha = norm_now / product
    direction, along = (residual, image)
    for sweep in range(ITERS):
        mesh_adjoint = mesh_adjoint + alpha * direction
        residual = residual - alpha * along
        if sweep + 1 < ITERS:
            image = operate(residual, shift)
            norm_next, product = two_products(residual, image)
            ratio = norm_next / norm_now
            alpha = norm_next / (product - ratio * norm_next / alpha)
            direction = residual + ratio * direction
            along = image + ratio * along
            norm_now = norm_next
    return (mesh_adjoint, residual)


def solution(mesh):
    placed = (
        P("inst", None, "cell", None, None),
        P("inst", None, None, "cell", None, None),
        P("cell", "inst", None),
    )
    return jax.shard_map(
        local,
        mesh=mesh,
        in_specs=placed,
        out_specs=(P(None, "cell", "inst", None), P(None, "cell", "inst", None)),
        check_vma=False,
    )
```

profile of v0, /device:TPU:0, one launch (start us, length us, event | category | flops | bytes accessed | tf_op | source)
XLA Modules:
  0.0 234.0 jit_solution(14785577434391238408)
XLA Ops:
  7.2 1.0 fusion.56
  8.2 1.3 collective-permute-start
  9.5 3.0 %collective-permute-start.1 = (bf16[2,5,1,16,256]{4,3,2,1,0:T(8,128)(2,1)S(1)}, bf16[2,5,1,16,256]{4,3,2,1,0:T(8,128)(2,1)S(1)}, u32[]{:S(2)}, u32[]{:S(2)}) collective-permute-start(bf16[2,5,1,16,256]{4,3,2,1,0:T(8,128)(2,1)S(1)} %get-tuple-element.22), channel_id=1, source_target_pairs={{0,1},{1,2},{2,3},{3,4},{4,5},{5,6},{6,7},{7,8},{8,9},{9,10},{10,1... | collective-permute-start | bytes 245768 | tf_op jit(solution)/shard_map/ppermute | solution.py:16
  12.6 0.9 collective-permute-done.1
  14.5 27.2 %all-reduce.8.cloned.1.call-done = f32[3,2,16,256]{3,2,1,0:T(8,128)} async-done(((f32[3,2,16,256]{3,2,1,0:T(8,128)}), f32[3,2,16,256]{3,2,1,0:T(8,128)}) %all-reduce.8.cloned.1.call-update) | async-done | bytes 98320 | tf_op jit(solution)/shard_map/psum | solution.py:71
  41.6 0.9 constant_dynamic-slice_fusion.1
  42.5 2.1 collective-permute-start.2
  44.6 1.3 collective-permute-start.3
  45.9 0.8 constant_dynamic-slice_fusion.2
  46.7 3.4 %collective-permute-done.3 = f32[3,2,1,256]{3,2,1,0:T(1,128)S(1)} collective-permute-done((f32[3,2,1,256]{3,2,1,0:T(1,128)S(1)}, f32[3,2,1,256]{3,2,1,0:T(1,128)S(1)}, u32[]{:S(2)}, u32[]{:S(2)}) %collective-permute-start.3) | collective-permute-done | bytes 6176 | tf_op jit(solution)/shard_map/ppermute | solution.py:19
  50.2 1.3 collective-permute-start.4
  51.5 3.0 %collective-permute-start.5 = (f32[3,1,10,256]{3,2,1,0:T(8,128)S(1)}, f32[3,1,10,256]{3,2,1,0:T(8,128)S(1)}, u32[]{:S(2)}, u32[]{:S(2)}) collective-permute-start(f32[3,1,10,256]{3,2,1,0:T(8,128)S(1)} %get-tuple-element.27), channel_id=1, source_target_pairs={{0,1},{1,2},{2,3},{3,4},{4,5},{5,6},{6,7},{7,8},{8,9},{9,10},{10,1... | collective-permute-start | bytes 92168 | tf_op jit(solution)/shard_map/ppermute | solution.py:16
  54.5 0.8 collective-permute-done.5
  56.4 0.7 multiply_reduce_fusion.4
  57.1 43.0 %all-reduce.5 = (f32[]{:T(128)}, f32[]{:T(128)}) all-reduce(f32[]{:T(128)} %get-tuple-element.9, f32[]{:T(128)} %get-tuple-element.8), channel_id=1, replica_groups=mesh['inst'=2,'cell'=16] {'inst','cell'}, use_global_device_ids=true, to_apply=%region_2.3 | all-reduce | flops 2 | bytes 16 | tf_op jit(solution)/shard_map/psum | solution.py:58
  101.4 4.4 %collective-permute-start.6 = (f32[3,2,1,256]{3,2,1,0:T(1,128)S(1)}, f32[3,2,1,256]{3,2,1,0:T(1,128)S(1)}, u32[]{:S(2)}, u32[]{:S(2)}) collective-permute-start(f32[3,2,1,256]{3,2,1,0:T(1,128)S(1)} %get-tuple-element.44), channel_id=1, source_target_pairs={{0,16},{1,17},{2,18},{3,19},{4,20},{5,21},{6,22},{7,23},{8,24},{9,... | collective-permute-start | bytes 18440 | tf_op jit(solution)/shard_map/ppermute | solution.py:16
  105.8 1.3 collective-permute-start.7
  107.1 4.2 %collective-permute-done.7 = f32[3,2,1,256]{3,2,1,0:T(1,128)S(1)} collective-permute-done((f32[3,2,1,256]{3,2,1,0:T(1,128)S(1)}, f32[3,2,1,256]{3,2,1,0:T(1,128)S(1)}, u32[]{:S(2)}, u32[]{:S(2)}) %collective-permute-start.7) | collective-permute-done | bytes 6176 | tf_op jit(solution)/shard_map/ppermute | solution.py:19
  111.4 1.3 collective-permute-start.8
  112.7 3.0 %collective-permute-start.9 = (f32[3,1,10,256]{3,2,1,0:T(8,128)S(1)}, f32[3,1,10,256]{3,2,1,0:T(8,128)S(1)}, u32[]{:S(2)}, u32[]{:S(2)}) collective-permute-start(f32[3,1,10,256]{3,2,1,0:T(8,128)S(1)} %get-tuple-element.25), channel_id=1, source_target_pairs={{0,1},{1,2},{2,3},{3,4},{4,5},{5,6},{6,7},{7,8},{8,9},{9,10},{10,1... | collective-permute-start | bytes 92168 | tf_op jit(solution)/shard_map/ppermute | solution.py:16
  115.7 0.9 collective-permute-done.9
  117.0 0.7 multiply_reduce_fusion.2
  117.7 42.4 %all-reduce.4 = (f32[]{:T(128)}, f32[]{:T(128)}) all-reduce(f32[]{:T(128)} %get-tuple-element.7, f32[]{:T(128)} %get-tuple-element.6), channel_id=1, replica_groups=mesh['inst'=2,'cell'=16] {'inst','cell'}, use_global_device_ids=true, to_apply=%region_6.7 | all-reduce | flops 2 | bytes 16 | tf_op jit(solution)/shard_map/psum | solution.py:58
  164.7 4.4 %collective-permute-start.10 = (f32[3,2,1,256]{3,2,1,0:T(1,128)S(1)}, f32[3,2,1,256]{3,2,1,0:T(1,128)S(1)}, u32[]{:S(2)}, u32[]{:S(2)}) collective-permute-start(f32[3,2,1,256]{3,2,1,0:T(1,128)S(1)} %get-tuple-element.42), channel_id=1, source_target_pairs={{0,16},{1,17},{2,18},{3,19},{4,20},{5,21},{6,22},{7,23},{8,24},{9,... | collective-permute-start | bytes 18440 | tf_op jit(solution)/shard_map/ppermute | solution.py:16
  169.2 1.3 collective-permute-start.11
  170.5 4.2 %collective-permute-done.11 = f32[3,2,1,256]{3,2,1,0:T(1,128)S(1)} collective-permute-done((f32[3,2,1,256]{3,2,1,0:T(1,128)S(1)}, f32[3,2,1,256]{3,2,1,0:T(1,128)S(1)}, u32[]{:S(2)}, u32[]{:S(2)}) %collective-permute-start.11) | collective-permute-done | bytes 6176 | tf_op jit(solution)/shard_map/ppermute | solution.py:19
  174.8 1.3 collective-permute-start.12
  176.1 3.0 %collective-permute-start.13 = (f32[3,1,10,256]{3,2,1,0:T(8,128)S(1)}, f32[3,1,10,256]{3,2,1,0:T(8,128)S(1)}, u32[]{:S(2)}, u32[]{:S(2)}) collective-permute-start(f32[3,1,10,256]{3,2,1,0:T(8,128)S(1)} %get-tuple-element.23), channel_id=1, source_target_pairs={{0,1},{1,2},{2,3},{3,4},{4,5},{5,6},{6,7},{7,8},{8,9},{9,10},{10,1... | collective-permute-start | bytes 92168 | tf_op jit(solution)/shard_map/ppermute | solution.py:16
  179.1 0.9 collective-permute-done.13
  180.3 0.7 multiply_reduce_fusion
  181.0 41.4 %all-reduce.3 = (f32[]{:T(128)}, f32[]{:T(128)}) all-reduce(f32[]{:T(128)} %get-tuple-element.5, f32[]{:T(128)} %get-tuple-element.4), channel_id=1, replica_groups=mesh['inst'=2,'cell'=16] {'inst','cell'}, use_global_device_ids=true, to_apply=%region_10.11 | all-reduce | flops 2 | bytes 16 | tf_op jit(solution)/shard_map/psum | solution.py:58
  226.5 0.7 multiply_subtract_fusion
  (42 shorter events, 3.0 us)
Async XLA Ops:
  7.2 6.3 %copy-start = (bf16[2,5,2,16,256]{4,3,2,1,0:T(8,128)(2,1)S(1)}, bf16[2,5,2,16,256]{4,3,2,1,0:T(8,128)(2,1)}, u32[]{:S(2)}) copy-start(bf16[2,5,2,16,256]{4,3,2,1,0:T(8,128)(2,1)} %param.3) | copy-start | bytes 491524
  7.2 34.5 %all-reduce.8.cloned.1.call-start = ((), (), s32[]{:S(2)}) async-start(), calls=%async_computation | async-start | bytes 196608 | tf_op jit(solution)/shard_map/psum | solution.py:71
  8.2 4.4 %collective-permute-start = (bf16[2,5,1,16,256]{4,3,2,1,0:T(8,128)(2,1)S(1)}, bf16[2,5,1,16,256]{4,3,2,1,0:T(8,128)(2,1)S(1)}, u32[]{:S(2)}, u32[]{:S(2)}) collective-permute-start(bf16[2,5,1,16,256]{4,3,2,1,0:T(8,128)(2,1)S(1)} %get-tuple-element.21), channel_id=1, source_target_pairs={{1,0},{2,1},{3,2},{4,3},{5,4},{6,5},{7,6},{8,7},{9,8},{10,9},{11,1... | collective-permute-start | bytes 245768 | tf_op jit(solution)/shard_map/ppermute | solution.py:19
  9.5 3.9 %collective-permute-start.1 = (bf16[2,5,1,16,256]{4,3,2,1,0:T(8,128)(2,1)S(1)}, bf16[2,5,1,16,256]{4,3,2,1,0:T(8,128)(2,1)S(1)}, u32[]{:S(2)}, u32[]{:S(2)}) collective-permute-start(bf16[2,5,1,16,256]{4,3,2,1,0:T(8,128)(2,1)S(1)} %get-tuple-element.22), channel_id=1, source_target_pairs={{0,1},{1,2},{2,3},{3,4},{4,5},{5,6},{6,7},{7,8},{8,9},{9,10},{10,1... | collective-permute-start | bytes 245768 | tf_op jit(solution)/shard_map/ppermute | solution.py:16
  12.6 1.0 copy-start.1
  42.5 4.2 %collective-permute-start.2 = (f32[3,2,1,256]{3,2,1,0:T(1,128)S(1)}, f32[3,2,1,256]{3,2,1,0:T(1,128)S(1)}, u32[]{:S(2)}, u32[]{:S(2)}) collective-permute-start(f32[3,2,1,256]{3,2,1,0:T(1,128)S(1)} %get-tuple-element.29), channel_id=1, source_target_pairs={{0,16},{1,17},{2,18},{3,19},{4,20},{5,21},{6,22},{7,23},{8,24},{9,... | collective-permute-start | bytes 18440 | tf_op jit(solution)/shard_map/ppermute | solution.py:16
  44.6 5.5 %collective-permute-start.3 = (f32[3,2,1,256]{3,2,1,0:T(1,128)S(1)}, f32[3,2,1,256]{3,2,1,0:T(1,128)S(1)}, u32[]{:S(2)}, u32[]{:S(2)}) collective-permute-start(f32[3,2,1,256]{3,2,1,0:T(1,128)S(1)} %get-tuple-element.30), channel_id=1, source_target_pairs={{16,0},{17,1},{18,2},{19,3},{20,4},{21,5},{22,6},{23,7},{24,8},{25... | collective-permute-start | bytes 18440 | tf_op jit(solution)/shard_map/ppermute | solution.py:19
  50.2 4.4 %collective-permute-start.4 = (f32[3,1,10,256]{3,2,1,0:T(8,128)S(1)}, f32[3,1,10,256]{3,2,1,0:T(8,128)S(1)}, u32[]{:S(2)}, u32[]{:S(2)}) collective-permute-start(f32[3,1,10,256]{3,2,1,0:T(8,128)S(1)} %get-tuple-element.28), channel_id=1, source_target_pairs={{1,0},{2,1},{3,2},{4,3},{5,4},{6,5},{7,6},{8,7},{9,8},{10,9},{11,1... | collective-permute-start | bytes 92168 | tf_op jit(solution)/shard_map/ppermute | solution.py:19
  51.5 3.9 %collective-permute-start.5 = (f32[3,1,10,256]{3,2,1,0:T(8,128)S(1)}, f32[3,1,10,256]{3,2,1,0:T(8,128)S(1)}, u32[]{:S(2)}, u32[]{:S(2)}) collective-permute-start(f32[3,1,10,256]{3,2,1,0:T(8,128)S(1)} %get-tuple-element.27), channel_id=1, source_target_pairs={{0,1},{1,2},{2,3},{3,4},{4,5},{5,6},{6,7},{7,8},{8,9},{9,10},{10,1... | collective-permute-start | bytes 92168 | tf_op jit(solution)/shard_map/ppermute | solution.py:16
  55.7 0.7 copy-start.3
  56.4 45.0 %copy-start.2 = (f32[3,2,16,256]{3,2,1,0:T(8,128)S(1)}, f32[3,2,16,256]{3,2,1,0:T(8,128)}, u32[]{:S(2)}) copy-start(f32[3,2,16,256]{3,2,1,0:T(8,128)} %all-reduce.8.cloned.1.call-done) | copy-start | bytes 294916
  101.4 5.7 %collective-permute-start.6 = (f32[3,2,1,256]{3,2,1,0:T(1,128)S(1)}, f32[3,2,1,256]{3,2,1,0:T(1,128)S(1)}, u32[]{:S(2)}, u32[]{:S(2)}) collective-permute-start(f32[3,2,1,256]{3,2,1,0:T(1,128)S(1)} %get-tuple-element.44), channel_id=1, source_target_pairs={{0,16},{1,17},{2,18},{3,19},{4,20},{5,21},{6,22},{7,23},{8,24},{9,... | collective-permute-start | bytes 18440 | tf_op jit(solution)/shard_map/ppermute | solution.py:16
  105.8 5.5 %collective-permute-start.7 = (f32[3,2,1,256]{3,2,1,0:T(1,128)S(1)}, f32[3,2,1,256]{3,2,1,0:T(1,128)S(1)}, u32[]{:S(2)}, u32[]{:S(2)}) collective-permute-start(f32[3,2,1,256]{3,2,1,0:T(1,128)S(1)} %get-tuple-element.45), channel_id=1, source_target_pairs={{16,0},{17,1},{18,2},{19,3},{20,4},{21,5},{22,6},{23,7},{24,8},{25... | collective-permute-start | bytes 18440 | tf_op jit(solution)/shard_map/ppermute | solution.py:19
  111.4 4.3 %collective-permute-start.8 = (f32[3,1,10,256]{3,2,1,0:T(8,128)S(1)}, f32[3,1,10,256]{3,2,1,0:T(8,128)S(1)}, u32[]{:S(2)}, u32[]{:S(2)}) collective-permute-start(f32[3,1,10,256]{3,2,1,0:T(8,128)S(1)} %get-tuple-element.26), channel_id=1, source_target_pairs={{1,0},{2,1},{3,2},{4,3},{5,4},{6,5},{7,6},{8,7},{9,8},{10,9},{11,1... | collective-permute-start | bytes 92168 | tf_op jit(solution)/shard_map/ppermute | solution.py:19
  112.7 3.9 %collective-permute-start.9 = (f32[3,1,10,256]{3,2,1,0:T(8,128)S(1)}, f32[3,1,10,256]{3,2,1,0:T(8,128)S(1)}, u32[]{:S(2)}, u32[]{:S(2)}) collective-permute-start(f32[3,1,10,256]{3,2,1,0:T(8,128)S(1)} %get-tuple-element.25), channel_id=1, source_target_pairs={{0,1},{1,2},{2,3},{3,4},{4,5},{5,6},{6,7},{7,8},{8,9},{9,10},{10,1... | collective-permute-start | bytes 92168 | tf_op jit(solution)/shard_map/ppermute | solution.py:16
  164.7 5.8 %collective-permute-start.10 = (f32[3,2,1,256]{3,2,1,0:T(1,128)S(1)}, f32[3,2,1,256]{3,2,1,0:T(1,128)S(1)}, u32[]{:S(2)}, u32[]{:S(2)}) collective-permute-start(f32[3,2,1,256]{3,2,1,0:T(1,128)S(1)} %get-tuple-element.42), channel_id=1, source_target_pairs={{0,16},{1,17},{2,18},{3,19},{4,20},{5,21},{6,22},{7,23},{8,24},{9,... | collective-permute-start | bytes 18440 | tf_op jit(solution)/shard_map/ppermute | solution.py:16
  169.2 5.5 %collective-permute-start.11 = (f32[3,2,1,256]{3,2,1,0:T(1,128)S(1)}, f32[3,2,1,256]{3,2,1,0:T(1,128)S(1)}, u32[]{:S(2)}, u32[]{:S(2)}) collective-permute-start(f32[3,2,1,256]{3,2,1,0:T(1,128)S(1)} %get-tuple-element.43), channel_id=1, source_target_pairs={{16,0},{17,1},{18,2},{19,3},{20,4},{21,5},{22,6},{23,7},{24,8},{25... | collective-permute-start | bytes 18440 | tf_op jit(solution)/shard_map/ppermute | solution.py:19
  174.8 4.3 %collective-permute-start.12 = (f32[3,1,10,256]{3,2,1,0:T(8,128)S(1)}, f32[3,1,10,256]{3,2,1,0:T(8,128)S(1)}, u32[]{:S(2)}, u32[]{:S(2)}) collective-permute-start(f32[3,1,10,256]{3,2,1,0:T(8,128)S(1)} %get-tuple-element.24), channel_id=1, source_target_pairs={{1,0},{2,1},{3,2},{4,3},{5,4},{6,5},{7,6},{8,7},{9,8},{10,9},{11,1... | collective-permute-start | bytes 92168 | tf_op jit(solution)/shard_map/ppermute | solution.py:19
  176.1 3.9 %collective-permute-start.13 = (f32[3,1,10,256]{3,2,1,0:T(8,128)S(1)}, f32[3,1,10,256]{3,2,1,0:T(8,128)S(1)}, u32[]{:S(2)}, u32[]{:S(2)}) collective-permute-start(f32[3,1,10,256]{3,2,1,0:T(8,128)S(1)} %get-tuple-element.23), channel_id=1, source_target_pairs={{0,1},{1,2},{2,3},{3,4},{4,5},{5,6},{6,7},{7,8},{8,9},{9,10},{10,1... | collective-permute-start | bytes 92168 | tf_op jit(solution)/shard_map/ppermute | solution.py:16
Sparse Core Ops, SparseCore 0:
  14.6 27.0 all-reduce.7
where the time goes:
time: 235 us; the launch traced here: 234 us
  blocking collectives  127 us (54%)
  waiting for transfers between devices  42.5 us (18%)
  starting transfers between devices  32.1 us (14%)
  between operations  24.4 us (10%)
  other arithmetic  4.82 us (2%)
  local copies, waits for them, and re-layouts  3.46 us (1%)
    psum x3, blocking collectives, two_products(): lax.psum((jnp.sum(residual * residual), jnp.sum(residual * image)), ('ins...  127 us
    psum x1, waiting for transfers between devices, local(): totals = lax.psum(partial_sum, 'inst')  27.2 us
    ppermute x7, starting transfers between devices, padded_2(): lax.ppermute(lax.slice_in_dim(block, block.shape[dim] - width, None, axis...  23 us
    ppermute x7, waiting for transfers between devices, padded_2(): lax.ppermute(lax.slice_in_dim(block, 0, width, axis=dim), axis, backward)  11.8 us
    ppermute x7, starting transfers between devices, padded_2(): lax.ppermute(lax.slice_in_dim(block, 0, width, axis=dim), axis, backward)  9.04 us
  transfers between devices with their start and end apart: 15, of which 8 were waited for; matrix products, arithmetic and copies ran while one was open for 0% of the time, Pallas kernels for 0%

commit v1 on v0

--- a/solution.py
+++ b/solution.py
@@ -68,7 +68,8 @@
     )
     partial_sum = upper - lower
     block_cols = shift.shape[1]
-    totals = lax.psum(partial_sum, "inst")
+    blocks = lax.all_gather(partial_sum, "inst")
+    totals = jnp.sum(blocks, axis=0)
     sens = lax.dynamic_slice_in_dim(totals, lax.axis_index("inst") * block_cols, block_cols, 2)
     mesh_adjoint = jnp.zeros_like(sens)
     residual = sens

time: 235 us -> 205 us (0.87)
  waiting for transfers between devices: 42.5 us -> 16 us
  between operations: 24.4 us -> 10.8 us
  blocking collectives: 127 us -> 136 us
    psum x1 -> x0, waiting for transfers between devices: 27.2 us -> none  [local(): totals = lax.psum(partial_sum, 'inst')]
    all_gather x0 -> x1, blocking collectives: none -> 6.25 us  [local(): blocks = lax.all_gather(partial_sum, 'inst')]
    psum x3, blocking collectives: 127 us -> 130 us  [two_products(): lax.psum((jnp.sum(residual * residual), jnp.sum(residual * image)), ('ins...]
  transfers between devices with their start and end apart: 15 -> 14, of which waited for: 8 -> 7; matrix products, arithmetic and copies ran while one was open for 0% -> 0% of each run, Pallas kernels for 0% -> 0%
where the time goes in v1:
time: 205 us; the launch traced here: 204 us
  blocking collectives  136 us (66%)
  starting transfers between devices  34.4 us (17%)
  waiting for transfers between devices  16 us (8%)
  between operations  10.8 us (5%)
  other arithmetic  4.22 us (2%)
    psum x3, blocking collectives, two_products(): lax.psum((jnp.sum(residual * residual), jnp.sum(residual * image)), ('ins...  130 us
    ppermute x7, starting transfers between devices, padded_2(): lax.ppermute(lax.slice_in_dim(block, block.shape[dim] - width, None, axis...  25.3 us
    ppermute x7, waiting for transfers between devices, padded_2(): lax.ppermute(lax.slice_in_dim(block, 0, width, axis=dim), axis, backward)  12.6 us
    ppermute x7, starting transfers between devices, padded_2(): lax.ppermute(lax.slice_in_dim(block, 0, width, axis=dim), axis, backward)  9.04 us
    all_gather x1, blocking collectives, local(): blocks = lax.all_gather(partial_sum, 'inst')  6.25 us
  transfers between devices with their start and end apart: 14, of which 7 were waited for; matrix products, arithmetic and copies ran while one was open for 0% of the time, Pallas kernels for 0%

profile of v1, /device:TPU:0, one launch (start us, length us, event | category | flops | bytes accessed | tf_op | source)
XLA Modules:
  0.0 203.6 jit_solution(17624733312936412429)
XLA Ops:
  0.6 1.0 fusion.56
  1.6 1.3 collective-permute-start
  2.9 3.0 %collective-permute-start.1 = (bf16[2,5,1,16,256]{4,3,2,1,0:T(8,128)(2,1)S(1)}, bf16[2,5,1,16,256]{4,3,2,1,0:T(8,128)(2,1)S(1)}, u32[]{:S(2)}, u32[]{:S(2)}) collective-permute-start(bf16[2,5,1,16,256]{4,3,2,1,0:T(8,128)(2,1)S(1)} %get-tuple-element.22), channel_id=1, source_target_pairs={{0,1},{1,2},{2,3},{3,4},{4,5},{5,6},{6,7},{7,8},{8,9},{9,10},{10,1... | collective-permute-start | bytes 245768 | tf_op jit(solution)/shard_map/ppermute | solution.py:16
  6.0 0.8 collective-permute-done.1
  7.2 6.3 %all-gather = f32[6,2,16,256]{3,2,1,0:T(8,128)S(1)} all-gather(f32[3,2,16,256]{3,2,1,0:T(8,128)S(1)} %subtract_bitcast_fusion), channel_id=2, replica_groups=mesh['inst'=2,'cell'=16] {'inst'}, dimensions={0}, use_global_device_ids=true | all-gather | bytes 294912 | tf_op jit(solution)/shard_map/all_gather | solution.py:71
  13.5 4.4 %collective-permute-start.2 = (f32[3,2,1,256]{3,2,1,0:T(1,128)S(1)}, f32[3,2,1,256]{3,2,1,0:T(1,128)S(1)}, u32[]{:S(2)}, u32[]{:S(2)}) collective-permute-start(f32[3,2,1,256]{3,2,1,0:T(1,128)S(1)} %get-tuple-element.29), channel_id=1, source_target_pairs={{0,16},{1,17},{2,18},{3,19},{4,20},{5,21},{6,22},{7,23},{8,24},{9,... | collective-permute-start | bytes 18440 | tf_op jit(solution)/shard_map/ppermute | solution.py:16
  17.9 1.3 collective-permute-start.3
  19.3 4.2 %collective-permute-done.3 = f32[3,2,1,256]{3,2,1,0:T(1,128)S(1)} collective-permute-done((f32[3,2,1,256]{3,2,1,0:T(1,128)S(1)}, f32[3,2,1,256]{3,2,1,0:T(1,128)S(1)}, u32[]{:S(2)}, u32[]{:S(2)}) %collective-permute-start.3) | collective-permute-done | bytes 6176 | tf_op jit(solution)/shard_map/ppermute | solution.py:19
  23.5 1.3 collective-permute-start.4
  24.8 3.0 %collective-permute-start.5 = (f32[3,1,10,256]{3,2,1,0:T(8,128)S(1)}, f32[3,1,10,256]{3,2,1,0:T(8,128)S(1)}, u32[]{:S(2)}, u32[]{:S(2)}) collective-permute-start(f32[3,1,10,256]{3,2,1,0:T(8,128)S(1)} %get-tuple-element.27), channel_id=1, source_target_pairs={{0,1},{1,2},{2,3},{3,4},{4,5},{5,6},{6,7},{7,8},{8,9},{9,10},{10,1... | collective-permute-start | bytes 92168 | tf_op jit(solution)/shard_map/ppermute | solution.py:16
  27.9 0.8 collective-permute-done.5
  28.7 0.2 select_maximum_fusion.8
  29.1 0.6 copy-done.2
  29.7 0.7 multiply_reduce_fusion.4
  30.4 46.4 %all-reduce.5 = (f32[]{:T(128)}, f32[]{:T(128)}) all-reduce(f32[]{:T(128)} %get-tuple-element.9, f32[]{:T(128)} %get-tuple-element.8), channel_id=1, replica_groups=mesh['inst'=2,'cell'=16] {'inst','cell'}, use_global_device_ids=true, to_apply=%region_2.3 | all-reduce | flops 2 | bytes 16 | tf_op jit(solution)/shard_map/psum | solution.py:58
  78.2 4.4 %collective-permute-start.6 = (f32[3,2,1,256]{3,2,1,0:T(1,128)S(1)}, f32[3,2,1,256]{3,2,1,0:T(1,128)S(1)}, u32[]{:S(2)}, u32[]{:S(2)}) collective-permute-start(f32[3,2,1,256]{3,2,1,0:T(1,128)S(1)} %get-tuple-element.44), channel_id=1, source_target_pairs={{0,16},{1,17},{2,18},{3,19},{4,20},{5,21},{6,22},{7,23},{8,24},{9,... | collective-permute-start | bytes 18440 | tf_op jit(solution)/shard_map/ppermute | solution.py:16
  82.5 1.3 collective-permute-start.7
  83.9 4.2 %collective-permute-done.7 = f32[3,2,1,256]{3,2,1,0:T(1,128)S(1)} collective-permute-done((f32[3,2,1,256]{3,2,1,0:T(1,128)S(1)}, f32[3,2,1,256]{3,2,1,0:T(1,128)S(1)}, u32[]{:S(2)}, u32[]{:S(2)}) %collective-permute-start.7) | collective-permute-done | bytes 6176 | tf_op jit(solution)/shard_map/ppermute | solution.py:19
  88.1 1.3 collective-permute-start.8
  89.4 3.0 %collective-permute-start.9 = (f32[3,1,10,256]{3,2,1,0:T(8,128)S(1)}, f32[3,1,10,256]{3,2,1,0:T(8,128)S(1)}, u32[]{:S(2)}, u32[]{:S(2)}) collective-permute-start(f32[3,1,10,256]{3,2,1,0:T(8,128)S(1)} %get-tuple-element.25), channel_id=1, source_target_pairs={{0,1},{1,2},{2,3},{3,4},{4,5},{5,6},{6,7},{7,8},{8,9},{9,10},{10,1... | collective-permute-start | bytes 92168 | tf_op jit(solution)/shard_map/ppermute | solution.py:16
  92.5 0.9 collective-permute-done.9
  93.7 0.7 multiply_reduce_fusion.2
  94.4 42.4 %all-reduce.4 = (f32[]{:T(128)}, f32[]{:T(128)}) all-reduce(f32[]{:T(128)} %get-tuple-element.7, f32[]{:T(128)} %get-tuple-element.6), channel_id=1, replica_groups=mesh['inst'=2,'cell'=16] {'inst','cell'}, use_global_device_ids=true, to_apply=%region_6.7 | all-reduce | flops 2 | bytes 16 | tf_op jit(solution)/shard_map/psum | solution.py:58
  141.4 4.4 %collective-permute-start.10 = (f32[3,2,1,256]{3,2,1,0:T(1,128)S(1)}, f32[3,2,1,256]{3,2,1,0:T(1,128)S(1)}, u32[]{:S(2)}, u32[]{:S(2)}) collective-permute-start(f32[3,2,1,256]{3,2,1,0:T(1,128)S(1)} %get-tuple-element.42), channel_id=1, source_target_pairs={{0,16},{1,17},{2,18},{3,19},{4,20},{5,21},{6,22},{7,23},{8,24},{9,... | collective-permute-start | bytes 18440 | tf_op jit(solution)/shard_map/ppermute | solution.py:16
  145.8 1.3 collective-permute-start.11
  147.1 4.2 %collective-permute-done.11 = f32[3,2,1,256]{3,2,1,0:T(1,128)S(1)} collective-permute-done((f32[3,2,1,256]{3,2,1,0:T(1,128)S(1)}, f32[3,2,1,256]{3,2,1,0:T(1,128)S(1)}, u32[]{:S(2)}, u32[]{:S(2)}) %collective-permute-start.11) | collective-permute-done | bytes 6176 | tf_op jit(solution)/shard_map/ppermute | solution.py:19
  151.4 1.3 collective-permute-start.12
  152.7 3.0 %collective-permute-start.13 = (f32[3,1,10,256]{3,2,1,0:T(8,128)S(1)}, f32[3,1,10,256]{3,2,1,0:T(8,128)S(1)}, u32[]{:S(2)}, u32[]{:S(2)}) collective-permute-start(f32[3,1,10,256]{3,2,1,0:T(8,128)S(1)} %get-tuple-element.23), channel_id=1, source_target_pairs={{0,1},{1,2},{2,3},{3,4},{4,5},{5,6},{6,7},{7,8},{8,9},{9,10},{10,1... | collective-permute-start | bytes 92168 | tf_op jit(solution)/shard_map/ppermute | solution.py:16
  155.7 0.9 collective-permute-done.13
  157.0 0.7 multiply_reduce_fusion
  157.7 41.4 %all-reduce.3 = (f32[]{:T(128)}, f32[]{:T(128)}) all-reduce(f32[]{:T(128)} %get-tuple-element.5, f32[]{:T(128)} %get-tuple-element.4), channel_id=1, replica_groups=mesh['inst'=2,'cell'=16] {'inst','cell'}, use_global_device_ids=true, to_apply=%region_10.11 | all-reduce | flops 2 | bytes 16 | tf_op jit(solution)/shard_map/psum | solution.py:58
  203.0 0.7 multiply_subtract_fusion
  (39 shorter events, 1.5 us)
Async XLA Ops:
  0.6 6.2 %copy-start = (bf16[2,5,2,16,256]{4,3,2,1,0:T(8,128)(2,1)S(1)}, bf16[2,5,2,16,256]{4,3,2,1,0:T(8,128)(2,1)}, u32[]{:S(2)}) copy-start(bf16[2,5,2,16,256]{4,3,2,1,0:T(8,128)(2,1)} %param.3) | copy-start | bytes 491524
  1.6 4.4 %collective-permute-start = (bf16[2,5,1,16,256]{4,3,2,1,0:T(8,128)(2,1)S(1)}, bf16[2,5,1,16,256]{4,3,2,1,0:T(8,128)(2,1)S(1)}, u32[]{:S(2)}, u32[]{:S(2)}) collective-permute-start(bf16[2,5,1,16,256]{4,3,2,1,0:T(8,128)(2,1)S(1)} %get-tuple-element.21), channel_id=1, source_target_pairs={{1,0},{2,1},{3,2},{4,3},{5,4},{6,5},{7,6},{8,7},{9,8},{10,9},{11,1... | collective-permute-start | bytes 245768 | tf_op jit(solution)/shard_map/ppermute | solution.py:19
  2.9 3.9 %collective-permute-start.1 = (bf16[2,5,1,16,256]{4,3,2,1,0:T(8,128)(2,1)S(1)}, bf16[2,5,1,16,256]{4,3,2,1,0:T(8,128)(2,1)S(1)}, u32[]{:S(2)}, u32[]{:S(2)}) collective-permute-start(bf16[2,5,1,16,256]{4,3,2,1,0:T(8,128)(2,1)S(1)} %get-tuple-element.22), channel_id=1, source_target_pairs={{0,1},{1,2},{2,3},{3,4},{4,5},{5,6},{6,7},{7,8},{8,9},{9,10},{10,1... | collective-permute-start | bytes 245768 | tf_op jit(solution)/shard_map/ppermute | solution.py:16
  6.0 1.0 copy-start.1
  13.5 5.7 %collective-permute-start.2 = (f32[3,2,1,256]{3,2,1,0:T(1,128)S(1)}, f32[3,2,1,256]{3,2,1,0:T(1,128)S(1)}, u32[]{:S(2)}, u32[]{:S(2)}) collective-permute-start(f32[3,2,1,256]{3,2,1,0:T(1,128)S(1)} %get-tuple-element.29), channel_id=1, source_target_pairs={{0,16},{1,17},{2,18},{3,19},{4,20},{5,21},{6,22},{7,23},{8,24},{9,... | collective-permute-start | bytes 18440 | tf_op jit(solution)/shard_map/ppermute | solution.py:16
  17.9 5.5 %collective-permute-start.3 = (f32[3,2,1,256]{3,2,1,0:T(1,128)S(1)}, f32[3,2,1,256]{3,2,1,0:T(1,128)S(1)}, u32[]{:S(2)}, u32[]{:S(2)}) collective-permute-start(f32[3,2,1,256]{3,2,1,0:T(1,128)S(1)} %get-tuple-element.30), channel_id=1, source_target_pairs={{16,0},{17,1},{18,2},{19,3},{20,4},{21,5},{22,6},{23,7},{24,8},{25... | collective-permute-start | bytes 18440 | tf_op jit(solution)/shard_map/ppermute | solution.py:19
  23.5 4.4 %collective-permute-start.4 = (f32[3,1,10,256]{3,2,1,0:T(8,128)S(1)}, f32[3,1,10,256]{3,2,1,0:T(8,128)S(1)}, u32[]{:S(2)}, u32[]{:S(2)}) collective-permute-start(f32[3,1,10,256]{3,2,1,0:T(8,128)S(1)} %get-tuple-element.28), channel_id=1, source_target_pairs={{1,0},{2,1},{3,2},{4,3},{5,4},{6,5},{7,6},{8,7},{9,8},{10,9},{11,1... | collective-permute-start | bytes 92168 | tf_op jit(solution)/shard_map/ppermute | solution.py:19
  24.8 3.9 %collective-permute-start.5 = (f32[3,1,10,256]{3,2,1,0:T(8,128)S(1)}, f32[3,1,10,256]{3,2,1,0:T(8,128)S(1)}, u32[]{:S(2)}, u32[]{:S(2)}) collective-permute-start(f32[3,1,10,256]{3,2,1,0:T(8,128)S(1)} %get-tuple-element.27), channel_id=1, source_target_pairs={{0,1},{1,2},{2,3},{3,4},{4,5},{5,6},{6,7},{7,8},{8,9},{9,10},{10,1... | collective-permute-start | bytes 92168 | tf_op jit(solution)/shard_map/ppermute | solution.py:16
  29.0 0.7 copy-start.2
  78.2 5.7 %collective-permute-start.6 = (f32[3,2,1,256]{3,2,1,0:T(1,128)S(1)}, f32[3,2,1,256]{3,2,1,0:T(1,128)S(1)}, u32[]{:S(2)}, u32[]{:S(2)}) collective-permute-start(f32[3,2,1,256]{3,2,1,0:T(1,128)S(1)} %get-tuple-element.44), channel_id=1, source_target_pairs={{0,16},{1,17},{2,18},{3,19},{4,20},{5,21},{6,22},{7,23},{8,24},{9,... | collective-permute-start | bytes 18440 | tf_op jit(solution)/shard_map/ppermute | solution.py:16
  82.5 5.5 %collective-permute-start.7 = (f32[3,2,1,256]{3,2,1,0:T(1,128)S(1)}, f32[3,2,1,256]{3,2,1,0:T(1,128)S(1)}, u32[]{:S(2)}, u32[]{:S(2)}) collective-permute-start(f32[3,2,1,256]{3,2,1,0:T(1,128)S(1)} %get-tuple-element.45), channel_id=1, source_target_pairs={{16,0},{17,1},{18,2},{19,3},{20,4},{21,5},{22,6},{23,7},{24,8},{25... | collective-permute-start | bytes 18440 | tf_op jit(solution)/shard_map/ppermute | solution.py:19
  88.1 4.3 %collective-permute-start.8 = (f32[3,1,10,256]{3,2,1,0:T(8,128)S(1)}, f32[3,1,10,256]{3,2,1,0:T(8,128)S(1)}, u32[]{:S(2)}, u32[]{:S(2)}) collective-permute-start(f32[3,1,10,256]{3,2,1,0:T(8,128)S(1)} %get-tuple-element.26), channel_id=1, source_target_pairs={{1,0},{2,1},{3,2},{4,3},{5,4},{6,5},{7,6},{8,7},{9,8},{10,9},{11,1... | collective-permute-start | bytes 92168 | tf_op jit(solution)/shard_map/ppermute | solution.py:19
  89.4 3.9 %collective-permute-start.9 = (f32[3,1,10,256]{3,2,1,0:T(8,128)S(1)}, f32[3,1,10,256]{3,2,1,0:T(8,128)S(1)}, u32[]{:S(2)}, u32[]{:S(2)}) collective-permute-start(f32[3,1,10,256]{3,2,1,0:T(8,128)S(1)} %get-tuple-element.25), channel_id=1, source_target_pairs={{0,1},{1,2},{2,3},{3,4},{4,5},{5,6},{6,7},{7,8},{8,9},{9,10},{10,1... | collective-permute-start | bytes 92168 | tf_op jit(solution)/shard_map/ppermute | solution.py:16
  141.4 5.8 %collective-permute-start.10 = (f32[3,2,1,256]{3,2,1,0:T(1,128)S(1)}, f32[3,2,1,256]{3,2,1,0:T(1,128)S(1)}, u32[]{:S(2)}, u32[]{:S(2)}) collective-permute-start(f32[3,2,1,256]{3,2,1,0:T(1,128)S(1)} %get-tuple-element.42), channel_id=1, source_target_pairs={{0,16},{1,17},{2,18},{3,19},{4,20},{5,21},{6,22},{7,23},{8,24},{9,... | collective-permute-start | bytes 18440 | tf_op jit(solution)/shard_map/ppermute | solution.py:16
  145.8 5.5 %collective-permute-start.11 = (f32[3,2,1,256]{3,2,1,0:T(1,128)S(1)}, f32[3,2,1,256]{3,2,1,0:T(1,128)S(1)}, u32[]{:S(2)}, u32[]{:S(2)}) collective-permute-start(f32[3,2,1,256]{3,2,1,0:T(1,128)S(1)} %get-tuple-element.43), channel_id=1, source_target_pairs={{16,0},{17,1},{18,2},{19,3},{20,4},{21,5},{22,6},{23,7},{24,8},{25... | collective-permute-start | bytes 18440 | tf_op jit(solution)/shard_map/ppermute | solution.py:19
  151.4 4.3 %collective-permute-start.12 = (f32[3,1,10,256]{3,2,1,0:T(8,128)S(1)}, f32[3,1,10,256]{3,2,1,0:T(8,128)S(1)}, u32[]{:S(2)}, u32[]{:S(2)}) collective-permute-start(f32[3,1,10,256]{3,2,1,0:T(8,128)S(1)} %get-tuple-element.24), channel_id=1, source_target_pairs={{1,0},{2,1},{3,2},{4,3},{5,4},{6,5},{7,6},{8,7},{9,8},{10,9},{11,1... | collective-permute-start | bytes 92168 | tf_op jit(solution)/shard_map/ppermute | solution.py:19
  152.7 3.9 %collective-permute-start.13 = (f32[3,1,10,256]{3,2,1,0:T(8,128)S(1)}, f32[3,1,10,256]{3,2,1,0:T(8,128)S(1)}, u32[]{:S(2)}, u32[]{:S(2)}) collective-permute-start(f32[3,1,10,256]{3,2,1,0:T(8,128)S(1)} %get-tuple-element.23), channel_id=1, source_target_pairs={{0,1},{1,2},{2,3},{3,4},{4,5},{5,6},{6,7},{7,8},{8,9},{9,10},{10,1... | collective-permute-start | bytes 92168 | tf_op jit(solution)/shard_map/ppermute | solution.py:16
